TPU v7x, 256 devices: a whole 4x4x8 slice. The times are simulated.
256 devices in a mesh: row: 8 (over y, core), col: 32 (over z, x).
Axes of the slice: x: 4, y: 4, z: 8, core: 2. Of those that a mesh axis runs over, the one named last changes fastest.
Arguments:
- ancestor: bfloat16 [16384, 16384], P('row', 'col'), may hold values from -6 to 6, as said below
- panels: bfloat16 [3, 512, 16384], P(None, 'col', 'row'), may hold values from -0.0625 to 0.0625
- diag_inverse: float32 [3, 512, 512], replicated, may hold values from -6 to 6, as said below
- supernode_blocks: int32 [3, 4], replicated, may hold values from 0 to 127, as said below
- row_lists: int32 [3, 64], replicated, may hold values from 0 to 127, as said below
Outputs:
- updated: bfloat16 [16384, 16384], P('row', 'col')
Inputs may be any that keep to these rules, and one draw needn't show every extreme that they name: ancestor is exactly symmetric. `diag_inverse`: each supernode's block is exactly symmetric. `supernode_blocks`: the 3 times 512 / 128 block numbers are all distinct. `row_lists`: each row holds 64 distinct block numbers; row s holds every block of the supernodes before s and none of supernode s or of later ones.
All inputs are finite; a program needn't handle non-finite values.
Results may differ from a plain program's by a relative error of at most 0.002.
Values may be sent and summed in bfloat16 or wider, within the bound.
No kernel may reach another device: no remote copies, remote signals or barrier semaphores. Data moves between devices by JAX's collectives and lax.ppermute only.
A program may use at most 64 MiB of HBM per device.

v0:
```python
import jax
import jax.numpy as jnp
from jax import lax
from jax.sharding import PartitionSpec as P

W = 512
B = 128
S = 3


def spread(value, axis, source):
    kept = jnp.where(lax.axis_index(axis) == source, value, 0).astype(value.dtype)
    return lax.psum(kept, axis)


def block_flags(listed, first_block, block_count):
    block_ids = first_block + jnp.arange(block_count, dtype=jnp.int32)
    return jnp.any(block_ids[:, None] == listed[None, :], axis=1)


def local(ancestor, panels, diag_inverse, supernode_blocks, row_lists):
    row_count = lax.axis_size("row")
    col_count = lax.axis_size("col")
    row_pos = lax.axis_index("row")
    col_pos = lax.axis_index("col")
    local_rows, local_cols = ancestor.shape
    per_node = W // B
    row_blocks = local_rows // B
    col_blocks = local_cols // B
    col_ratio = col_count // row_count
    first_rowblock = row_pos * row_blocks
    first_colblock = col_pos * col_blocks
    current = ancestor
    for supernode in range(S):
        listed = row_lists[supernode]
        owned_blocks = supernode_blocks[supernode]
        row_flags = block_flags(listed, first_rowblock, row_blocks)
        col_flags = block_flags(listed, first_colblock, col_blocks)
        panel_rows = lax.all_gather(panels[supernode], "col", axis=0, tiled=True)
        panel_rows = jnp.where(
            row_flags[None, :, None], panel_rows.reshape(W, row_blocks, B), 0
        ).reshape(W, local_rows)
        partial_value = -lax.dot_general(
            current, panel_rows, (((0,), (1,)), ((), ())), preferred_element_type=jnp.float32
        )
        col_sum = lax.psum(partial_value, "row")
        col_update = (
            jnp.where(col_flags[:, None, None], col_sum.reshape(col_blocks, B, W), 0.0)
            .reshape(local_cols, W)
            .astype(jnp.bfloat16)
        )
        slab_list = [
            spread(col_update, "col", col_ratio * row_pos + shift_idx)
            for shift_idx in range(col_ratio)
        ]
        row_update = jnp.concatenate(slab_list, axis=0)
        cross_part = jnp.dot(panel_rows, row_update, preferred_element_type=jnp.float32)
        cross_term = lax.psum(cross_part.astype(jnp.bfloat16), "row").astype(jnp.float32)
        diag_block = (diag_inverse[supernode] - 0.5 * (cross_term + cross_term.T)).astype(
            jnp.bfloat16
        )
        col_match = (first_colblock + jnp.arange(col_blocks, dtype=jnp.int32))[
            :, None
        ] == owned_blocks[None, :]
        row_match = (first_rowblock + jnp.arange(row_blocks, dtype=jnp.int32))[
            :, None
        ] == owned_blocks[None, :]
        col_hit = jnp.any(col_match, axis=1)
        row_hit = jnp.any(row_match, axis=1)
        col_select = col_match.astype(jnp.bfloat16)
        row_select = row_match.astype(jnp.bfloat16)
        column_fill = jnp.einsum(
            "rkb,jk->rjb",
            row_update.reshape(local_rows, per_node, B),
            col_select,
            preferred_element_type=jnp.float32,
        ).astype(jnp.bfloat16)
        blocks_view = jnp.where(
            col_hit[None, :, None], column_fill, current.reshape(local_rows, col_blocks, B)
        )
        row_fill = jnp.einsum(
            "jkb,ik->ibj",
            col_update.reshape(local_cols, per_node, B),
            row_select,
            preferred_element_type=jnp.float32,
        ).astype(jnp.bfloat16)
        rows_view = jnp.where(
            row_hit[:, None, None], row_fill, blocks_view.reshape(row_blocks, B, local_cols)
        )
        corner = jnp.einsum(
            "ik,kalb,jl->iajb",
            row_select,
            diag_block.reshape(per_node, B, per_node, B),
            col_select,
            preferred_element_type=jnp.float32,
        ).astype(jnp.bfloat16)
        corner_hit = row_hit[:, None, None, None] & col_hit[None, None, :, None]
        grid_view = jnp.where(corner_hit, corner, rows_view.reshape(row_blocks, B, col_blocks, B))
        current = grid_view.reshape(local_rows, local_cols)
    return current


def solution(mesh):
    in_specs = (P("row", "col"), P(None, "col", "row"), P(), P(), P())
    out_specs = P("row", "col")
    return jax.shard_map(local, mesh=mesh, in_specs=in_specs, out_specs=out_specs, check_vma=False)
```

profile of v0, /device:TPU:2, one launch (start us, length us, event | category | flops | bytes accessed | tf_op | source)
XLA Modules:
  0.0 1100.6 jit_solution(17126207968095562700)
XLA Ops:
  9.6 79.9 %all-gather.11.cloned.1.call-done = bf16[1,512,2048]{2,1,0:T(8,128)(2,1)} async-done(((bf16[1,16,2048]{2,1,0:T(8,128)(2,1)}), bf16[1,512,2048]{2,1,0:T(8,128)(2,1)}) %all-gather.11.cloned.1.call-update) | async-done | bytes 2097168 | tf_op jit(solution)/shard_map/all_gather | solution.py:39
  89.5 3.5 fusion.11
  93.0 50.2 %all-reduce.24 = bf16[512,512]{0,1:T(8,128)(2,1)S(1)} all-reduce(f32[512,512]{0,1:T(8,128)S(1)} %fusion.11), channel_id=1, replica_groups=mesh['row'=8,'col'=32] {'row'}, use_global_device_ids=true, to_apply=%region_12.13 | all-reduce | flops 262144 | bytes 1572864 | tf_op jit(solution)/shard_map/psum | solution.py:46
  145.5 152.2 %all-reduce.23.cloned.1.call-done = (bf16[512,512]{0,1:T(8,128)(2,1)}, bf16[512,512]{0,1:T(8,128)(2,1)}, bf16[512,512]{0,1:T(8,128)(2,1)}, bf16[512,512]{0,1:T(8,128)(2,1)}) async-done(((bf16[512,512]{0,1:T(8,128)(2,1)}, bf16[512,512]{0,1:T(8,128)(2,1)}, bf16[512,512]{0,1:T(8,128)(2,1)}, bf16[512,512]{0,1:T(8,128)(2,1)}), (bf16[512,512]{0,1:T(8,128)(2,1)}, bf16[512,512]{0,1:T(8,128)(2,1)}, ...) | async-done | bytes 2097168 | tf_op jit(solution)/shard_map/psum | solution.py:13
  303.0 4.0 reshape.191
  307.8 2.6 copy.55
  310.4 3.8 bitcast_select_fusion.6
  316.4 3.4 copy.95
  322.2 5.1 copy.58
  327.3 40.0 %all-reduce.13.cloned.1.call-done = bf16[512,512]{1,0:T(8,128)(2,1)} async-done(((bf16[512,512]{1,0:T(8,128)(2,1)}), bf16[512,512]{1,0:T(8,128)(2,1)}) %all-reduce.13.cloned.1.call-update) | async-done | bytes 524304 | tf_op jit(solution)/shard_map/psum | solution.py:58
  370.9 2.6 bitcast_select_fusion.8
  373.5 3.7 copy.59
  377.2 68.5 %all-gather.9.cloned.1.call-done = bf16[1,512,2048]{2,1,0:T(8,128)(2,1)} async-done(((bf16[1,16,2048]{2,1,0:T(8,128)(2,1)}), bf16[1,512,2048]{2,1,0:T(8,128)(2,1)}) %all-gather.9.cloned.1.call-update) | async-done | bytes 2097168 | tf_op jit(solution)/shard_map/all_gather | solution.py:39
  445.7 4.5 fusion.12
  450.2 51.0 %all-reduce.25 = bf16[512,512]{0,1:T(8,128)(2,1)S(1)} all-reduce(f32[512,512]{0,1:T(8,128)} %fusion.12), channel_id=1, replica_groups=mesh['row'=8,'col'=32] {'row'}, use_global_device_ids=true, to_apply=%region_18.19 | all-reduce | flops 262144 | bytes 1572864 | tf_op jit(solution)/shard_map/psum | solution.py:46
  503.4 152.1 %all-reduce.21.cloned.1.call-done = (bf16[512,512]{0,1:T(8,128)(2,1)}, bf16[512,512]{0,1:T(8,128)(2,1)}, bf16[512,512]{0,1:T(8,128)(2,1)}, bf16[512,512]{0,1:T(8,128)(2,1)}) async-done(((bf16[512,512]{0,1:T(8,128)(2,1)}, bf16[512,512]{0,1:T(8,128)(2,1)}, bf16[512,512]{0,1:T(8,128)(2,1)}, bf16[512,512]{0,1:T(8,128)(2,1)}), (bf16[512,512]{0,1:T(8,128)(2,1)}, bf16[512,512]{0,1:T(8,128)(2,1)}, ...) | async-done | bytes 2097168 | tf_op jit(solution)/shard_map/psum | solution.py:13
  664.7 4.4 copy.65
  669.1 5.2 bitcast_select_fusion.3
  674.3 4.1 reshape.223
  678.4 3.4 copy.98
  684.2 5.1 copy.70
  689.3 37.2 %all-reduce.15.cloned.1.call-done = bf16[512,512]{0,1:T(8,128)(2,1)} async-done(((bf16[512,512]{0,1:T(8,128)(2,1)}), bf16[512,512]{0,1:T(8,128)(2,1)}) %all-reduce.15.cloned.1.call-update) | async-done | bytes 524304 | tf_op jit(solution)/shard_map/psum | solution.py:58
  732.7 3.7 copy.71
  736.4 68.6 %all-gather.7.cloned.1.call-done = bf16[1,512,2048]{2,1,0:T(8,128)(2,1)} async-done(((bf16[1,16,2048]{2,1,0:T(8,128)(2,1)}), bf16[1,512,2048]{2,1,0:T(8,128)(2,1)}) %all-gather.7.cloned.1.call-update) | async-done | bytes 2097168 | tf_op jit(solution)/shard_map/all_gather | solution.py:39
  805.0 4.5 fusion.15
  809.5 50.8 %all-reduce.26 = bf16[512,512]{0,1:T(8,128)(2,1)S(1)} all-reduce(f32[512,512]{0,1:T(8,128)} %fusion.15), channel_id=1, replica_groups=mesh['row'=8,'col'=32] {'row'}, use_global_device_ids=true, to_apply=%region_24.25 | all-reduce | flops 262144 | bytes 1572864 | tf_op jit(solution)/shard_map/psum | solution.py:46
  865.1 149.7 %all-reduce.19.cloned.1.call-done = (bf16[512,512]{0,1:T(8,128)(2,1)}, bf16[512,512]{0,1:T(8,128)(2,1)}, bf16[512,512]{0,1:T(8,128)(2,1)}, bf16[512,512]{0,1:T(8,128)(2,1)}) async-done(((bf16[512,512]{0,1:T(8,128)(2,1)}, bf16[512,512]{0,1:T(8,128)(2,1)}, bf16[512,512]{0,1:T(8,128)(2,1)}, bf16[512,512]{0,1:T(8,128)(2,1)}), (bf16[512,512]{0,1:T(8,128)(2,1)}, bf16[512,512]{0,1:T(8,128)(2,1)}, ...) | async-done | bytes 2097168 | tf_op jit(solution)/shard_map/psum | solution.py:13
  1019.5 2.6 copy.77
  1022.0 4.5 bitcast_select_fusion
  1028.8 3.4 copy.101
  1034.6 4.2 copy.82
  1038.8 45.6 %all-reduce.17.cloned.1.call-done = bf16[512,512]{0,1:T(8,128)(2,1)} async-done(((bf16[512,512]{0,1:T(8,128)(2,1)}), bf16[512,512]{0,1:T(8,128)(2,1)}) %all-reduce.17.cloned.1.call-update) | async-done | bytes 524304 | tf_op jit(solution)/shard_map/psum | solution.py:58
  (106 shorter events, 62.5 us)
Async XLA Ops:
  6.5 83.0 %all-gather.11.cloned.1.call-start = ((), (), s32[]{:S(2)}) async-start(), calls=%async_computation.5 | async-start | bytes 2162688 | tf_op jit(solution)/shard_map/all_gather | solution.py:39
  8.1 289.5 %all-reduce.23.cloned.1.call-start = ((), (), s32[]{:S(2)}) async-start(), calls=%async_computation.8 | async-start | bytes 4194304 | tf_op jit(solution)/shard_map/psum | solution.py:13
  145.4 222.0 %all-reduce.13.cloned.1.call-start = ((), (), s32[]{:S(2)}) async-start(), calls=%async_computation | async-start | bytes 1048576 | tf_op jit(solution)/shard_map/psum | solution.py:58
  297.6 2.4 copy-start.6
  297.6 2.5 copy-start.4
  297.6 2.5 copy-start.9
  302.3 143.4 %all-gather.9.cloned.1.call-start = ((), (), s32[]{:S(2)}) async-start(), calls=%async_computation.4 | async-start | bytes 2162688 | tf_op jit(solution)/shard_map/all_gather | solution.py:39
  302.9 4.0 copy-start.8
  302.9 352.6 %all-reduce.21.cloned.1.call-start = ((), (), s32[]{:S(2)}) async-start(), calls=%async_computation.7 | async-start | bytes 4194304 | tf_op jit(solution)/shard_map/psum | solution.py:13
  503.4 223.2 %all-reduce.15.cloned.1.call-start = ((), (), s32[]{:S(2)}) async-start(), calls=%async_computation.1 | async-start | bytes 1048576 | tf_op jit(solution)/shard_map/psum | solution.py:58
  655.6 2.4 copy-start.7
  655.6 2.4 copy-start.5
  655.6 3.8 copy-start.10
  658.1 1.3 copy-start
  661.5 143.5 %all-gather.7.cloned.1.call-start = ((), (), s32[]{:S(2)}) async-start(), calls=%async_computation.3 | async-start | bytes 2162688 | tf_op jit(solution)/shard_map/all_gather | solution.py:39
  662.3 352.5 %all-reduce.19.cloned.1.call-start = ((), (), s32[]{:S(2)}) async-start(), calls=%async_computation.6 | async-start | bytes 4194304 | tf_op jit(solution)/shard_map/psum | solution.py:13
  664.7 4.4 copy-start.1
  862.6 221.9 %all-reduce.17.cloned.1.call-start = ((), (), s32[]{:S(2)}) async-start(), calls=%async_computation.2 | async-start | bytes 1048576 | tf_op jit(solution)/shard_map/psum | solution.py:58
  1014.8 2.4 copy-start.3
  1014.8 2.5 copy-start.2
  1014.8 2.5 copy-start.11
Sparse Core Ops, SparseCore 0:
  9.9 79.5 all-gather.10
  145.5 152.0 all-reduce.22
  302.4 64.8 all-reduce.12
  369.8 75.8 all-gather.8
  503.5 152.0 all-reduce.20
  661.6 64.8 all-reduce.14
  729.2 75.8 all-gather.6
  862.7 152.0 all-reduce.18
  1019.6 64.8 all-reduce.16
where the time goes:
time: 1100 us
  waiting for transfers between devices  795 us (72%)
  blocking collectives  152 us (14%)
  local copies, waits for them, and re-layouts  79 us (7%)
  matrix products  47 us (4%)
  between operations  13.6 us (1%)
  other arithmetic  13.1 us (1%)
    psum x3, waiting for transfers between devices, spread(): return lax.psum(kept, axis)  454 us
    all_gather x3, waiting for transfers between devices, local(): panel_rows = lax.all_gather(panels[supernode], 'col', axis=0, tiled=True)  217 us
    psum x3, blocking collectives, local(): col_sum = lax.psum(partial_value, 'row')  152 us
    psum x3, waiting for transfers between devices, local(): lax.psum(cross_part.astype(jnp.bfloat16), 'row').astype(jnp.float32)  123 us
  transfers between devices with their start and end apart: 9, of which 9 were waited for; matrix products, arithmetic and copies ran while one was open for 9% of the time, Pallas kernels for 0%

commit v1 on v0

--- a/solution.py
+++ b/solution.py
@@ -55,7 +55,11 @@
         ]
         row_update = jnp.concatenate(slab_list, axis=0)
         cross_part = jnp.dot(panel_rows, row_update, preferred_element_type=jnp.float32)
-        cross_term = lax.psum(cross_part.astype(jnp.bfloat16), "row").astype(jnp.float32)
+
+        def steps_all_view(block_here):
+            return jnp.sum(lax.all_gather(block_here, "row"), axis=0)
+
+        cross_term = steps_all_view(cross_part.astype(jnp.bfloat16)).astype(jnp.float32)
         diag_block = (diag_inverse[supernode] - 0.5 * (cross_term + cross_term.T)).astype(
             jnp.bfloat16
         )

time: 1100 us -> 1020 us (0.927)
  waiting for transfers between devices: 795 us -> 680 us
  local copies, waits for them, and re-layouts: 79 us -> 96.8 us
    psum x3 -> x0, waiting for transfers between devices: 123 us -> none  [local(): lax.psum(cross_part.astype(jnp.bfloat16), 'row').astype(jnp.float32)]
  transfers between devices with their start and end apart: 9 -> 9, of which waited for: 9 -> 8; matrix products, arithmetic and copies ran while one was open for 9% -> 11% of each run, Pallas kernels for 0% -> 0%
where the time goes in v1:
time: 1020 us; the launch traced here: 1010 us
  waiting for transfers between devices  680 us (67%)
  blocking collectives  152 us (15%)
  local copies, waits for them, and re-layouts  96.8 us (9%)
  matrix products  49.5 us (5%)
  other arithmetic  19.8 us (2%)
  between operations  13.9 us (1%)
    psum x3, waiting for transfers between devices, spread(): return lax.psum(kept, axis)  456 us
    all_gather x3, waiting for transfers between devices, local(): panel_rows = lax.all_gather(panels[supernode], 'col', axis=0, tiled=True)  216 us
    psum x3, blocking collectives, local(): col_sum = lax.psum(partial_value, 'row')  152 us
    reshape x6, local copies, waits for them, and re-layouts, local(): blocks_view.reshape(row_blocks, B, local_cols)  22.9 us
  transfers between devices with their start and end apart: 9, of which 8 were waited for; matrix products, arithmetic and copies ran while one was open for 11% of the time, Pallas kernels for 0%

profile of v1, /device:TPU:2, one launch (start us, length us, event | category | flops | bytes accessed | tf_op | source)
XLA Modules:
  0.0 1013.6 jit_solution(11961366595848299)
XLA Ops:
  9.6 80.0 %all-gather.17.cloned.1.call-done = bf16[1,512,2048]{2,1,0:T(8,128)(2,1)} async-done(((bf16[1,16,2048]{2,1,0:T(8,128)(2,1)}), bf16[1,512,2048]{2,1,0:T(8,128)(2,1)}) %all-gather.17.cloned.1.call-update) | async-done | bytes 2097168 | tf_op jit(solution)/shard_map/all_gather | solution.py:39
  89.6 3.5 fusion.11
  93.0 50.2 %all-reduce.15 = bf16[512,512]{0,1:T(8,128)(2,1)S(1)} all-reduce(f32[512,512]{0,1:T(8,128)S(1)} %fusion.11), channel_id=1, replica_groups=mesh['row'=8,'col'=32] {'row'}, use_global_device_ids=true, to_apply=%region_12.13 | all-reduce | flops 262144 | bytes 1572864 | tf_op jit(solution)/shard_map/psum | solution.py:46
  145.5 152.1 %all-reduce.14.cloned.1.call-done = (bf16[512,512]{0,1:T(8,128)(2,1)}, bf16[512,512]{0,1:T(8,128)(2,1)}, bf16[512,512]{0,1:T(8,128)(2,1)}, bf16[512,512]{0,1:T(8,128)(2,1)}) async-done(((bf16[512,512]{0,1:T(8,128)(2,1)}, bf16[512,512]{0,1:T(8,128)(2,1)}, bf16[512,512]{0,1:T(8,128)(2,1)}, bf16[512,512]{0,1:T(8,128)(2,1)}), (bf16[512,512]{0,1:T(8,128)(2,1)}, bf16[512,512]{0,1:T(8,128)(2,1)}, ...) | async-done | bytes 2097168 | tf_op jit(solution)/shard_map/psum | solution.py:13
  306.8 3.5 fusion.72
  312.6 4.5 copy.92
  317.0 4.5 bitcast_select_fusion.6
  321.5 4.2 reshape.225
  325.7 3.5 copy.130
  329.2 3.4 bitcast_select_fusion.7
  332.6 5.1 copy.95
  344.9 3.7 copy.96
  348.7 67.5 %all-gather.15.cloned.1.call-done = bf16[1,512,2048]{2,1,0:T(8,128)(2,1)} async-done(((bf16[1,16,2048]{2,1,0:T(8,128)(2,1)}), bf16[1,512,2048]{2,1,0:T(8,128)(2,1)}) %all-gather.15.cloned.1.call-update) | async-done | bytes 2097168 | tf_op jit(solution)/shard_map/all_gather | solution.py:39
  416.2 4.5 fusion.12
  420.7 50.8 %all-reduce.16 = bf16[512,512]{0,1:T(8,128)(2,1)S(1)} all-reduce(f32[512,512]{0,1:T(8,128)} %fusion.12), channel_id=1, replica_groups=mesh['row'=8,'col'=32] {'row'}, use_global_device_ids=true, to_apply=%region_18.19 | all-reduce | flops 262144 | bytes 1572864 | tf_op jit(solution)/shard_map/psum | solution.py:46
  473.7 152.3 %all-reduce.12.cloned.1.call-done = (bf16[512,512]{0,1:T(8,128)(2,1)}, bf16[512,512]{0,1:T(8,128)(2,1)}, bf16[512,512]{0,1:T(8,128)(2,1)}, bf16[512,512]{0,1:T(8,128)(2,1)}) async-done(((bf16[512,512]{0,1:T(8,128)(2,1)}, bf16[512,512]{0,1:T(8,128)(2,1)}, bf16[512,512]{0,1:T(8,128)(2,1)}, bf16[512,512]{0,1:T(8,128)(2,1)}), (bf16[512,512]{0,1:T(8,128)(2,1)}, bf16[512,512]{0,1:T(8,128)(2,1)}, ...) | async-done | bytes 2097168 | tf_op jit(solution)/shard_map/psum | solution.py:13
  637.9 4.4 copy.102
  642.3 5.4 bitcast_select_fusion.3
  647.6 4.1 reshape.226
  651.8 3.5 copy.133
  657.6 5.2 copy.107
  672.6 3.7 copy.108
  676.3 68.2 %all-gather.13.cloned.1.call-done = bf16[1,512,2048]{2,1,0:T(8,128)(2,1)} async-done(((bf16[1,16,2048]{2,1,0:T(8,128)(2,1)}), bf16[1,512,2048]{2,1,0:T(8,128)(2,1)}) %all-gather.13.cloned.1.call-update) | async-done | bytes 2097168 | tf_op jit(solution)/shard_map/all_gather | solution.py:39
  744.6 4.5 fusion.15
  749.1 50.8 %all-reduce.17 = bf16[512,512]{0,1:T(8,128)(2,1)S(1)} all-reduce(f32[512,512]{0,1:T(8,128)} %fusion.15), channel_id=1, replica_groups=mesh['row'=8,'col'=32] {'row'}, use_global_device_ids=true, to_apply=%region_24.25 | all-reduce | flops 262144 | bytes 1572864 | tf_op jit(solution)/shard_map/psum | solution.py:46
  802.3 152.0 %all-reduce.10.cloned.1.call-done = (bf16[512,512]{0,1:T(8,128)(2,1)}, bf16[512,512]{0,1:T(8,128)(2,1)}, bf16[512,512]{0,1:T(8,128)(2,1)}, bf16[512,512]{0,1:T(8,128)(2,1)}) async-done(((bf16[512,512]{0,1:T(8,128)(2,1)}, bf16[512,512]{0,1:T(8,128)(2,1)}, bf16[512,512]{0,1:T(8,128)(2,1)}, bf16[512,512]{0,1:T(8,128)(2,1)}), (bf16[512,512]{0,1:T(8,128)(2,1)}, bf16[512,512]{0,1:T(8,128)(2,1)}, ...) | async-done | bytes 2097168 | tf_op jit(solution)/shard_map/psum | solution.py:13
  965.1 4.4 copy.114
  969.5 5.3 bitcast_select_fusion
  974.9 4.1 reshape.227
  979.0 3.4 copy.136
  984.8 4.3 copy.119
  989.0 4.6 all-gather.23.cloned.1.call-done
  (128 shorter events, 78.5 us)
Async XLA Ops:
  6.5 83.0 %all-gather.17.cloned.1.call-start = ((), (), s32[]{:S(2)}) async-start(), calls=%async_computation.2 | async-start | bytes 2162688 | tf_op jit(solution)/shard_map/all_gather | solution.py:39
  8.1 289.5 %all-reduce.14.cloned.1.call-start = ((), (), s32[]{:S(2)}) async-start(), calls=%async_computation.8 | async-start | bytes 4194304 | tf_op jit(solution)/shard_map/psum | solution.py:13
  145.5 192.3 %all-gather.19.cloned.1.call-start = ((), (), s32[]{:S(2)}) async-start(), calls=%async_computation.3 | async-start | bytes 4718592 | tf_op jit(solution)/shard_map/all_gather | solution.py:60
  297.6 2.4 copy-start.11
  297.6 2.5 copy-start.8
  297.6 3.9 copy-start.16
  300.2 1.3 copy-start.1
  301.5 3.2 copy-start.4
  303.6 112.5 %all-gather.15.cloned.1.call-start = ((), (), s32[]{:S(2)}) async-start(), calls=%async_computation.1 | async-start | bytes 2162688 | tf_op jit(solution)/shard_map/all_gather | solution.py:39
  304.2 321.8 %all-reduce.12.cloned.1.call-start = ((), (), s32[]{:S(2)}) async-start(), calls=%async_computation.7 | async-start | bytes 4194304 | tf_op jit(solution)/shard_map/psum | solution.py:13
  310.2 0.7 copy-start.14
  312.6 4.5 copy-start.5
  473.6 191.7 %all-gather.21.cloned.1.call-start = ((), (), s32[]{:S(2)}) async-start(), calls=%async_computation.4 | async-start | bytes 4718592 | tf_op jit(solution)/shard_map/all_gather | solution.py:60
  626.0 2.4 copy-start.12
  626.0 2.5 copy-start.9
  626.0 3.9 copy-start.15
  628.5 1.3 copy-start.2
  631.9 112.6 %all-gather.13.cloned.1.call-start = ((), (), s32[]{:S(2)}) async-start(), calls=%async_computation | async-start | bytes 2162688 | tf_op jit(solution)/shard_map/all_gather | solution.py:39
  632.7 321.6 %all-reduce.10.cloned.1.call-start = ((), (), s32[]{:S(2)}) async-start(), calls=%async_computation.6 | async-start | bytes 4194304 | tf_op jit(solution)/shard_map/psum | solution.py:13
  637.8 4.4 copy-start.6
  665.3 3.4 copy-start
  802.1 191.6 %all-gather.23.cloned.1.call-start = ((), (), s32[]{:S(2)}) async-start(), calls=%async_computation.5 | async-start | bytes 4718592 | tf_op jit(solution)/shard_map/all_gather | solution.py:60
  954.3 2.4 copy-start.13
  954.3 2.5 copy-start.10
  954.3 3.9 copy-start.17
  956.8 1.3 copy-start.3
  965.1 4.4 copy-start.7
Sparse Core Ops, SparseCore 0:
  9.9 79.6 all-gather.16
  145.6 151.9 all-reduce.13
  303.8 33.2 all-gather.18
  339.5 76.6 all-gather.14
  473.8 152.1 all-reduce.11
  632.1 33.2 all-gather.20
  667.9 76.6 all-gather.12
  802.2 152.0 all-reduce.9
  960.4 33.2 all-gather.22
